TPU v7x, 32 devices: a whole 2x2x4 slice. The times are simulated.
32 devices in a mesh: dp: 4 (over z), tensor: 4 (over y, x), section: 2 (over core).
Axes of the slice: x: 2, y: 2, z: 4, core: 2. Of those that a mesh axis runs over, the one named last changes fastest.
Arguments:
- grads: bfloat16 [4, 2, 768, 768], P('dp', 'section', 'tensor'), may hold values from -6 to 6
- errors: float32 [4, 2, 768, 768], P('dp', 'section', 'tensor'), may hold values from -3 to 3
- q_prev: float32 [2, 768, 32], P('section'), may hold values from -0.21875 to 0.21875
- p_root: float32 [2, 32, 32], P('section')
- q_root: float32 [2, 32, 32], P('section')
- momentum: float32 [2, 768, 768], P('section', 'tensor')
- weights: float32 [2, 768, 768], P('section', 'tensor'), may hold values from -0.21875 to 0.21875
- vec_grads: float32 [4, 2, 3, 768], P('dp', 'section', None, 'tensor'), may hold values from -6 to 6
- vec_momentum: float32 [2, 3, 768], P('section', None, 'tensor'), may hold values from -6 to 6
- vec_params: float32 [2, 3, 768], P('section', None, 'tensor'), may hold values from -3 to 3
Outputs:
- errors_out: float32 [4, 2, 768, 768], P('dp', 'section', 'tensor')
- p_factor: float32 [2, 768, 32], P('section', 'tensor')
- q_factor: float32 [2, 768, 32], P('section')
- momentum_out: float32 [2, 768, 768], P('section', 'tensor')
- weights_out: float32 [2, 768, 768], P('section', 'tensor')
- vec_momentum_out: float32 [2, 3, 768], P('section', None, 'tensor')
- vec_params_out: float32 [2, 3, 768], P('section', None, 'tensor')
All inputs are finite; a program needn't handle non-finite values.
Results may differ from a plain program's by a relative error of at most 0.0003.
Values sent between devices are 32-bit elements; how exact they have to be, the bound alone decides.
A program may use at most 64 MiB of HBM per device.

v0:
```python
import jax
import jax.numpy as jnp
from jax import lax
from jax.sharding import PartitionSpec as P

D = 768


HIGH = lax.Precision.HIGHEST


def shards(
    grads, errors, q_prev, p_root, q_root, momentum, weights, vec_grads, vec_momentum, vec_params
):
    replicas = lax.axis_size("dp")
    vec_local = vec_grads[0, 0]
    vec_sum = lax.psum(vec_local, "dp")
    merged = grads[0, 0].astype(jnp.float32) + errors[0, 0]
    p_local = jnp.dot(merged, q_prev[0], precision=HIGH, preferred_element_type=jnp.float32)
    p_sum = lax.psum(p_local, "dp")
    p_factor = jnp.dot(p_sum, p_root[0], precision=HIGH, preferred_element_type=jnp.float32)
    q_partial = lax.dot_general(
        merged,
        p_factor,
        (((0,), (0,)), ((), ())),
        precision=HIGH,
        preferred_element_type=jnp.float32,
    )
    q_whole = lax.psum(q_partial, ("dp", "tensor"))
    q_factor = jnp.dot(q_whole, q_root[0], precision=HIGH, preferred_element_type=jnp.float32)
    approx = (
        lax.dot_general(
            p_factor,
            q_factor,
            (((1,), (1,)), ((), ())),
            precision=HIGH,
            preferred_element_type=jnp.float32,
        )
        / replicas
    )
    errors_out = merged - approx
    vec_mean = vec_sum / replicas
    momentum_out = 0.9 * momentum[0] + approx
    vec_momentum_out = 0.9 * vec_momentum[0] + vec_mean
    local_total = jnp.sum(momentum_out * momentum_out) + jnp.sum(
        vec_momentum_out * vec_momentum_out
    )
    total = lax.psum(local_total, ("tensor", "section"))
    scale = 0.05 / jnp.sqrt(total / (2 * D * D + 6 * D) + 1e-06)
    weights_out = weights[0] - scale * momentum_out
    vec_params_out = vec_params[0] - scale * vec_momentum_out
    return (
        errors_out[None, None],
        p_factor[None],
        q_factor[None],
        momentum_out[None],
        weights_out[None],
        vec_momentum_out[None],
        vec_params_out[None],
    )


def solution(mesh):
    in_specs = (
        P("dp", "section", "tensor", None),
        P("dp", "section", "tensor", None),
        P("section", None, None),
        P("section", None, None),
        P("section", None, None),
        P("section", "tensor", None),
        P("section", "tensor", None),
        P("dp", "section", None, "tensor"),
        P("section", None, "tensor"),
        P("section", None, "tensor"),
    )
    out_specs = (
        P("dp", "section", "tensor", None),
        P("section", "tensor", None),
        P("section", None, None),
        P("section", "tensor", None),
        P("section", "tensor", None),
        P("section", None, "tensor"),
        P("section", None, "tensor"),
    )
    return jax.shard_map(shards, mesh=mesh, in_specs=in_specs, out_specs=out_specs, check_vma=False)
```

profile of v0, /device:TPU:0, one launch (start us, length us, event | category | flops | bytes accessed | tf_op | source)
XLA Modules:
  0.0 168.7 jit_solution(3444834635649647149)
XLA Ops:
  7.2 0.0 copy-start
  7.2 0.0 all-reduce.3.cloned.1.call-start
  7.2 0.7 copy.26
  7.9 0.2 copy-done
  8.1 0.0 copy-start.1
  8.1 0.0 copy-start.2
  8.1 1.8 %fusion.3 = f32[192,32]{1,0:T(8,128)S(1)} fusion(f32[1,1,192,768]{3,2,1,0:T(8,128)} %param.11, bf16[1,1,192,768]{3,2,1,0:T(8,128)(2,1)} %param.10, f32[1,768,32]{1,2,0:T(8,128)S(1)} %copy-done), kind=kOutput, calls=%fused_computation.7 | convolution fusion | flops 56918016 | bytes 1007616 | tf_op jit(solution)/shard_map/dot_general | solution.py:19
  9.9 0.0 copy-start.7
  9.9 22.7 %all-reduce = (f32[192,32]{1,0:T(8,128)S(1)}, f32[3,192]{1,0:T(4,128)S(1)}) all-reduce(f32[192,32]{1,0:T(8,128)S(1)} %fusion.3, f32[3,192]{1,0:T(4,128)S(1)} %bitcast.52), channel_id=1, replica_groups=mesh['dp'=4,'tensor'=4,'section'=2] {'dp'}, use_global_device_ids=true, to_apply=%region_0.0 | all-reduce | flops 6720 | bytes 53760 | tf_op jit(solution)/shard_map/psum | solution.py:20
  32.6 0.0 copy-done.7
  32.6 0.3 fusion.9
  32.9 0.0 copy-done.1
  32.9 0.0 copy-done.2
  32.9 0.0 copy-start.6
  32.9 0.0 copy-start.9
  33.0 0.0 copy-start.8
  33.0 2.2 %fusion.1 = f32[768,32]{1,0:T(8,128)} fusion(f32[192,32]{0,1:T(8,128)S(1)} %fusion.9, f32[1,1,192,768]{3,2,1,0:T(8,128)S(1)} %copy-done.1, bf16[1,1,192,768]{3,2,1,0:T(8,128)(2,1)S(1)} %copy-done.2), kind=kOutput, calls=%fused_computation.5 | convolution fusion | flops 56918016 | bytes 1007616 | tf_op jit(solution)/shard_map/dot_general | solution.py:22
  35.2 0.0 copy-start.3
  35.2 0.0 all-reduce.3.cloned.1.call-update
  35.2 0.0 copy-done.9
  35.2 0.6 multiply_reduce_fusion.1
  35.8 105.7 %all-reduce.3.cloned.1.call-done = f32[768,32]{1,0:T(8,128)} async-done(((f32[768,32]{1,0:T(8,128)}), f32[768,32]{1,0:T(8,128)}) %all-reduce.3.cloned.1.call-update) | async-done | bytes 98320 | tf_op jit(solution)/shard_map/psum | solution.py:29
  141.5 0.0 copy-done.8
  141.5 1.5 fusion.7
  143.1 0.0 copy-done.6
  143.1 0.0 copy-done.3
  143.1 0.0 copy-start.5
  143.1 0.0 copy-start.4
  143.1 1.4 multiply_reduce_fusion
  144.5 0.0 copy-done.5
  145.8 0.6 broadcast_in_dim.26
  146.4 12.3 %psum.31 = f32[]{:T(128)} all-reduce(f32[]{:T(128)S(6)} %add.31), channel_id=1, replica_groups=mesh['dp'=4,'tensor'=4,'section'=2] {'tensor','section'}, use_global_device_ids=true, to_apply=%region_5.0 | all-reduce | flops 1 | bytes 8 | tf_op jit(solution)/shard_map/psum | solution.py:48
  159.3 0.0 copy-start.10
  159.3 0.6 copy-done.10
  160.0 0.6 broadcast_in_dim.27
  160.6 0.0 copy-done.4
  160.6 1.3 fusion
  (1 shorter events, 0.0 us)
Async XLA Ops:
  7.2 0.9 copy-start
  7.2 134.4 %all-reduce.3.cloned.1.call-start = ((), (), s32[]{:S(2)}) async-start(), calls=%async_computation | async-start | bytes 786432 | tf_op jit(solution)/shard_map/psum | solution.py:29
  8.1 24.8 %copy-start.1 = (f32[1,1,192,768]{3,2,1,0:T(8,128)S(1)}, f32[1,1,192,768]{3,2,1,0:T(8,128)}, u32[]{:S(2)}) copy-start(f32[1,1,192,768]{3,2,1,0:T(8,128)} %param.11) | copy-start | bytes 1769476
  8.1 24.9 %copy-start.2 = (bf16[1,1,192,768]{3,2,1,0:T(8,128)(2,1)S(1)}, bf16[1,1,192,768]{3,2,1,0:T(8,128)(2,1)}, u32[]{:S(2)}) copy-start(bf16[1,1,192,768]{3,2,1,0:T(8,128)(2,1)} %param.10) | copy-start | bytes 884740
  9.9 22.7 %copy-start.7 = (f32[1,32,32]{2,1,0:T(8,128)S(1)}, f32[1,32,32]{2,1,0:T(8,128)}, u32[]{:S(2)}) copy-start(f32[1,32,32]{2,1,0:T(8,128)} %param.13) | copy-start | bytes 12292
  32.9 110.1 %copy-start.6 = (f32[192,32]{0,1:T(8,128)}, f32[192,32]{0,1:T(8,128)S(1)}, u32[]{:S(2)}) copy-start(f32[192,32]{0,1:T(8,128)S(1)} %fusion.9) | copy-start | bytes 73732
  32.9 2.3 %copy-start.9 = (f32[1,3,192]{2,0,1:T(1,128)S(1)}, f32[1,3,192]{2,0,1:T(1,128)}, u32[]{:S(2)}) copy-start(f32[1,3,192]{2,0,1:T(1,128)} %param.18) | copy-start | bytes 6916
  33.0 108.6 %copy-start.8 = (f32[1,32,32]{2,1,0:T(8,128)S(1)}, f32[1,32,32]{2,1,0:T(8,128)}, u32[]{:S(2)}) copy-start(f32[1,32,32]{2,1,0:T(8,128)} %param.14) | copy-start | bytes 12292
  35.2 107.9 %copy-start.3 = (f32[1,192,768]{2,1,0:T(8,128)S(1)}, f32[1,192,768]{2,1,0:T(8,128)}, u32[]{:S(2)}) copy-start(f32[1,192,768]{2,1,0:T(8,128)} %param.15) | copy-start | bytes 1769476
  143.1 1.4 copy-start.5
  143.1 17.5 %copy-start.4 = (f32[1,192,768]{2,1,0:T(8,128)S(1)}, f32[1,192,768]{2,1,0:T(8,128)}, u32[]{:S(2)}) copy-start(f32[1,192,768]{2,1,0:T(8,128)} %param.16) | copy-start | bytes 1769476
  159.3 0.7 copy-start.10
Sparse Core Ops, SparseCore 0:
  35.3 106.1 all-reduce.2
where the time goes:
time: 169 us
  waiting for transfers between devices  106 us (63%)
  blocking collectives  35 us (21%)
  between operations  16.2 us (10%)
  matrix products  7.21 us (4%)
  local copies, waits for them, and re-layouts  2.7 us (2%)
  other arithmetic  1.89 us (1%)
    psum x1, waiting for transfers between devices, shards(): q_whole = lax.psum(q_partial, ('dp', 'tensor'))  106 us
    psum x1, blocking collectives, shards(): p_sum = lax.psum(p_local, 'dp')  22.7 us
    psum x1, blocking collectives, shards(): total = lax.psum(local_total, ('tensor', 'section'))  12.3 us
  transfers between devices with their start and end apart: 1, of which 1 were waited for; matrix products, arithmetic and copies ran while one was open for 0% of the time, Pallas kernels for 0%

commit v1 on v0

v1 whole, which is shorter than its diff:
```python
import functools

import jax
import jax.numpy as jnp
from jax import lax
from jax.experimental import pallas as pl
from jax.experimental.pallas import tpu as pltpu
from jax.sharding import PartitionSpec as P

F32 = jnp.float32
BF16 = jnp.bfloat16
MESH = pl.DeviceIdType.MESH
CHUNK_ROWS = 16
CHUNK_COLS = 128


def split(x):
    high = x.astype(BF16)
    return high, (x - high.astype(F32)).astype(BF16)


def mm(a, b, dims=((1,), (0,))):
    return lax.dot_general(a, b, (dims, ((), ())), preferred_element_type=F32)


def left_parts(x):
    high, low = split(x)
    return jnp.concatenate([high, high, low], axis=1)


def right_parts(x):
    high, low = split(x)
    return jnp.concatenate([high, low, high], axis=0)


def each(count, body):
    if count <= 16:
        for i in range(count):
            body(i)
    else:
        lax.fori_loop(0, count, lambda i, c: (body(i), c)[1], 0)


def kernel(
    sizes,
    g_hbm, e_hbm, qt_hbm, pr_hbm, qr_hbm, m_hbm, w_hbm, vg_hbm, vm_hbm, vp_hbm,
    eo_hbm, pt_hbm, qf_hbm, mo_hbm, wo_hbm, vmo_hbm, vpo_hbm,
    g_v, e_v, qt_v, pr_v, qr_v, m_v, w_v, vm_v, vp_v,
    hi_v, lo_v, pbuf, vbuf, qpart, rbuf, qfull, sbuf, pf_v, qf_v,
    in_sem, out_sem, psend, precv, vsend, vrecv, rsend, rrecv, asend, arecv, ssend, srecv,
):
    n_dp, n_t, n_s = sizes
    n = n_dp * n_t
    group = n_t * n_s
    dp, tn, sc = lax.axis_index("dp"), lax.axis_index("tensor"), lax.axis_index("section")
    me = dp * n_t + tn
    rank, width = qt_v.shape
    rows = e_v.shape[0]
    col_chunks = width // CHUNK_COLS
    chunks = (rank // CHUNK_ROWS) * col_chunks
    mine = (me * chunks + n - 1) // n
    owns = jnp.logical_and(mine < chunks, (mine * n) // chunks == me)

    def load(i, src, dst):
        copy = pltpu.make_async_copy(src, dst, in_sem.at[i])
        copy.start()
        return copy

    ins = [
        load(0, g_hbm, g_v),
        load(1, e_hbm, e_v),
        load(2, qt_hbm, qt_v),
        load(3, pr_hbm, pr_v),
        load(4, qr_hbm, qr_v),
        load(5, vg_hbm, vbuf.at[dp]),
        load(6, m_hbm, m_v),
        load(7, vm_hbm, vm_v),
        load(8, w_hbm, w_v),
        load(9, vp_hbm, vp_v),
    ]

    barrier = pltpu.get_barrier_semaphore()

    def greet_group(i):
        peer = lax.rem(me + 1 + i, n)
        pl.semaphore_signal(
            barrier, inc=1, device_id=(peer // n_t, lax.rem(peer, n_t), sc), device_id_type=MESH
        )

    def greet_section(i):
        other = lax.rem(sc + 1 + i // n_t, n_s)
        pl.semaphore_signal(
            barrier, inc=1, device_id=(dp, i % n_t, other), device_id_type=MESH
        )

    each(n - 1, greet_group)
    each((n_s - 1) * n_t, greet_section)

    ins[2].wait()
    q_hi, q_lo = split(qt_v[...])
    ins[0].wait()
    ins[1].wait()
    merged = g_v[...].astype(F32) + e_v[...]
    e_v[...] = merged
    m_hi, m_lo = split(merged)
    hi_v[...] = m_hi
    lo_v[...] = m_lo
    first = mm(jnp.concatenate([q_hi, q_lo], axis=0), hi_v[...], ((1,), (1,)))
    second = mm(q_hi, lo_v[...], ((1,), (1,)))
    pbuf[dp] = first[:rank] + first[rank:] + second

    pl.semaphore_wait(barrier, n - 1 + (n_s - 1) * n_t)
    ins[5].wait()

    def send_p(i):
        peer = lax.rem(dp + 1 + i, n_dp)
        pltpu.make_async_remote_copy(
            pbuf.at[dp], pbuf.at[dp], psend, precv, device_id=(peer, tn, sc), device_id_type=MESH
        ).start()

    def send_v(i):
        peer = lax.rem(dp + 1 + i, n_dp)
        pltpu.make_async_remote_copy(
            vbuf.at[dp], vbuf.at[dp], vsend, vrecv, device_id=(peer, tn, sc), device_id_type=MESH
        ).start()

    each(n_dp - 1, send_p)
    each(n_dp - 1, send_v)

    ins[3].wait()
    ins[4].wait()
    p_root_left = left_parts(pr_v[...].T)
    q_root_left = left_parts(qr_v[...])

    others = pl.ds(0, n_dp - 1)
    pltpu.make_async_copy(pbuf.at[others], pbuf.at[others], precv).wait()
    if n_dp <= 16:
        p_sum = pbuf[0]
        for i in range(1, n_dp):
            p_sum = p_sum + pbuf[i]
    else:
        p_sum = lax.fori_loop(1, n_dp, lambda i, acc: acc + pbuf[i], pbuf[0])
    pf = mm(p_root_left, right_parts(p_sum))
    pf_hi, pf_lo = split(pf)
    pf_both = jnp.concatenate([pf_hi, pf_lo], axis=0)

    def send_chunk(k):
        owner = (k * n) // chunks
        at = (
            pl.ds((k // col_chunks) * CHUNK_ROWS, CHUNK_ROWS),
            pl.ds((k % col_chunks) * CHUNK_COLS, CHUNK_COLS),
        )

        @pl.when(me == owner)
        def _():
            rbuf[me] = qpart[at]

        @pl.when(me != owner)
        def _():
            pltpu.make_async_remote_copy(
                qpart.at[at], rbuf.at[me], rsend, rrecv,
                device_id=(owner // n_t, owner % n_t, sc), device_id_type=MESH,
            ).start()

    block = 2 * CHUNK_COLS
    for c in range(width // block):
        cols = pl.ds(c * block, block)
        first = mm(pf_both, hi_v[:, cols])
        second = mm(pf_hi, lo_v[:, cols])
        qpart[:, cols] = first[:rank] + first[rank:] + second
    for k in range(chunks):
        send_chunk(k)

    pf_v[...] = pf
    p_out = pltpu.make_async_copy(pf_v, pt_hbm, out_sem.at[0])
    p_out.start()
    left = mm(q_root_left, right_parts(pf)).T / n_dp
    left = left_parts(left)

    pltpu.make_async_copy(vbuf.at[others], vbuf.at[others], vrecv).wait()
    if n_dp <= 16:
        v_sum = vbuf[0]
        for i in range(1, n_dp):
            v_sum = v_sum + vbuf[i]
    else:
        v_sum = lax.fori_loop(1, n_dp, lambda i, acc: acc + vbuf[i], vbuf[0])
    ins[7].wait()
    v_new = 0.9 * vm_v[...] + v_sum / n_dp
    vm_v[...] = v_new
    v_out = pltpu.make_async_copy(vm_v, vmo_hbm, out_sem.at[1])
    v_out.start()
    v_square = jnp.sum(v_new * v_new)

    @pl.when(owns)
    def _():
        whole = pl.ds(0, n - 1)
        pltpu.make_async_copy(rbuf.at[whole], rbuf.at[whole], rrecv).wait()
        if n <= 16:
            q_sum = rbuf[0]
            for i in range(1, n):
                q_sum = q_sum + rbuf[i]
        else:
            q_sum = lax.fori_loop(1, n, lambda i, acc: acc + rbuf[i], rbuf[0])
        qfull[mine] = q_sum

        def send_sum(i):
            peer = lax.rem(me + 1 + i, n)
            pltpu.make_async_remote_copy(
                qfull.at[mine], qfull.at[mine], asend, arecv,
                device_id=(peer // n_t, lax.rem(peer, n_t), sc), device_id_type=MESH,
            ).start()

        each(n - 1, send_sum)
        got = pl.ds(0, chunks - 1)
        pltpu.make_async_copy(qfull.at[got], qfull.at[got], arecv).wait()

    @pl.when(jnp.logical_not(owns))
    def _():
        pltpu.make_async_copy(qfull, qfull, arecv).wait()

    ins[6].wait()
    squares = jnp.zeros((8, 128), F32)
    q_parts = []
    for c in range(width // block):
        cols = pl.ds(c * block, block)
        q_sum = jnp.concatenate(
            [
                jnp.concatenate([qfull[r * col_chunks + 2 * c + j] for j in range(2)], axis=1)
                for r in range(rank // CHUNK_ROWS)
            ],
            axis=0,
        )
        right = right_parts(q_sum)
        q_parts.append(right)
        approx = mm(left, right)
        new = 0.9 * m_v[:, cols] + approx
        m_v[:, cols] = new
        e_v[:, cols] = e_v[:, cols] - approx
        square = new * new
        for j in range(2):
            squares = squares + jnp.sum(
                square[:, j * 128 : (j + 1) * 128].reshape(rows // 8, 8, 128), axis=0
            )
    corner = jnp.logical_and(
        lax.broadcasted_iota(jnp.int32, (8, 128), 0) == 0,
        lax.broadcasted_iota(jnp.int32, (8, 128), 1) == 0,
    )
    slot = sc * n_t + tn
    sbuf[slot] = squares + jnp.where(corner, v_square, 0.0)
    for i in range(1, group):
        peer = lax.rem(slot + i, group)
        pltpu.make_async_remote_copy(
            sbuf.at[slot], sbuf.at[slot], ssend, srecv,
            device_id=(dp, lax.rem(peer, n_t), peer // n_t), device_id_type=MESH,
        ).start()
    m_out = pltpu.make_async_copy(m_v, mo_hbm, out_sem.at[2])
    m_out.start()
    e_out = pltpu.make_async_copy(e_v, eo_hbm, out_sem.at[3])
    e_out.start()
    q_root_t = left_parts(qr_v[...].T)
    for c in range(width // block):
        qf_v[:, pl.ds(c * block, block)] = mm(q_root_t, q_parts[c])
    q_out = pltpu.make_async_copy(qf_v, qf_hbm, out_sem.at[4])
    q_out.start()
    ins[8].wait()
    ins[9].wait()

    rest = pl.ds(0, group - 1)
    pltpu.make_async_copy(sbuf.at[rest], sbuf.at[rest], srecv).wait()
    total_tile = sbuf[0]
    for i in range(1, group):
        total_tile = total_tile + sbuf[i]
    total = jnp.sum(jnp.sum(total_tile, axis=1, keepdims=True), axis=0, keepdims=True)
    count = n_s * (width * width + 3 * width)
    scale = 0.05 / jnp.sqrt(total / count + 1e-06)
    outs = [p_out, v_out, m_out, e_out, q_out]
    pieces = 4
    step = rows // pieces
    for i in range(pieces):
        part = pl.ds(i * step, step)
        w_v[part, :] = w_v[part, :] - scale * m_v[part, :]
        copy = pltpu.make_async_copy(w_v.at[part], wo_hbm.at[part], out_sem.at[5 + i])
        copy.start()
        outs.append(copy)
    vp_v[...] = vp_v[...] - scale.reshape(1, 1, 1) * vm_v[...]
    copy = pltpu.make_async_copy(vp_v, vpo_hbm, out_sem.at[5 + pieces])
    copy.start()
    outs.append(copy)

    pltpu.make_async_copy(pbuf.at[others], pbuf.at[others], psend).wait()
    pltpu.make_async_copy(vbuf.at[others], vbuf.at[others], vsend).wait()
    pltpu.make_async_copy(sbuf.at[rest], sbuf.at[rest], ssend).wait()

    @pl.when(owns)
    def _():
        got = pl.ds(0, chunks - 1)
        pltpu.make_async_copy(qfull.at[got], qfull.at[got], rsend).wait()
        whole = pl.ds(0, n - 1)
        pltpu.make_async_copy(rbuf.at[whole], rbuf.at[whole], asend).wait()

    @pl.when(jnp.logical_not(owns))
    def _():
        pltpu.make_async_copy(qfull, qfull, rsend).wait()

    for copy in outs:
        copy.wait()


def shards(
    sizes,
    grads, errors, q_prev, p_root, q_root, momentum, weights, vec_grads, vec_momentum, vec_params,
):
    n_dp, n_t, n_s = sizes
    rows, width = errors.shape[2:]
    rank = q_prev.shape[2]
    vecs, entries = vec_params.shape[1:]
    n = n_dp * n_t
    chunks = (rank // CHUNK_ROWS) * (width // CHUNK_COLS)
    big = jax.ShapeDtypeStruct((rows, width), F32)
    vec = jax.ShapeDtypeStruct((vecs, 1, entries), F32)
    any_space = pl.BlockSpec(memory_space=pl.ANY)
    dma = pltpu.SemaphoreType.DMA
    vmem = pltpu.VMEM
    outs = pl.pallas_call(
        functools.partial(kernel, sizes),
        out_shape=(
            big,
            jax.ShapeDtypeStruct((rank, rows), F32),
            jax.ShapeDtypeStruct((rank, width), F32),
            big,
            big,
            vec,
            vec,
        ),
        in_specs=[pl.BlockSpec(memory_space=pltpu.HBM)] * 10,
        out_specs=(any_space,) * 7,
        scratch_shapes=[
            vmem((rows, width), BF16),
            vmem((rows, width), F32),
            vmem((rank, width), F32),
            vmem((rank, rank), F32),
            vmem((rank, rank), F32),
            vmem((rows, width), F32),
            vmem((rows, width), F32),
            vmem((vecs, 1, entries), F32),
            vmem((vecs, 1, entries), F32),
            vmem((rows, width), BF16),
            vmem((rows, width), BF16),
            vmem((n_dp, rank, rows), F32),
            vmem((n_dp, vecs, 1, entries), F32),
            vmem((rank, width), F32),
            vmem((n, CHUNK_ROWS, CHUNK_COLS), F32),
            vmem((chunks, CHUNK_ROWS, CHUNK_COLS), F32),
            vmem((n_t * n_s, 8, 128), F32),
            vmem((rank, rows), F32),
            vmem((rank, width), F32),
            dma((10,)),
            dma((10,)),
        ]
        + [dma(())] * 10,
        compiler_params=pltpu.CompilerParams(
            collective_id=0, has_side_effects=True, vmem_limit_bytes=48 * 1024 * 1024
        ),
    )(
        grads[0, 0],
        errors[0, 0],
        q_prev[0].T,
        p_root[0],
        q_root[0],
        momentum[0],
        weights[0],
        vec_grads[0, 0][:, None, :],
        vec_momentum[0][:, None, :],
        vec_params[0][:, None, :],
    )
    errors_out, p_factor, q_factor, momentum_out, weights_out, vec_momentum_out, vec_params_out = outs
    return (
        errors_out[None, None],
        p_factor.T[None],
        q_factor.T[None],
        momentum_out[None],
        weights_out[None],
        vec_momentum_out[:, 0][None],
        vec_params_out[:, 0][None],
    )


def solution(mesh):
    sizes = (mesh.shape["dp"], mesh.shape["tensor"], mesh.shape["section"])
    in_specs = (
        P("dp", "section", "tensor", None),
        P("dp", "section", "tensor", None),
        P("section", None, None),
        P("section", None, None),
        P("section", None, None),
        P("section", "tensor", None),
        P("section", "tensor", None),
        P("dp", "section", None, "tensor"),
        P("section", None, "tensor"),
        P("section", None, "tensor"),
    )
    out_specs = (
        P("dp", "section", "tensor", None),
        P("section", "tensor", None),
        P("section", None, None),
        P("section", "tensor", None),
        P("section", "tensor", None),
        P("section", None, "tensor"),
        P("section", None, "tensor"),
    )
    return jax.shard_map(
        functools.partial(shards, sizes),
        mesh=mesh, in_specs=in_specs, out_specs=out_specs, check_vma=False,
    )
```

time: 169 us -> 40.7 us (0.24)
  waiting for transfers between devices: 106 us -> 0 us
  blocking collectives: 35 us -> 0 us
  Pallas kernels: 0 us -> 26.2 us
  between operations: 16.2 us -> 0.67 us
  local copies, waits for them, and re-layouts: 2.7 us -> 13.4 us
  matrix products: 7.21 us -> 0 us
  other arithmetic: 1.89 us -> 0 us
    psum x1 -> x0, waiting for transfers between devices: 106 us -> none  [shards(): q_whole = lax.psum(q_partial, ('dp', 'tensor'))]
    psum x2 -> x0, blocking collectives: 35 us -> none  [the longest x1 22.7 us: shards(): p_sum = lax.psum(p_local, 'dp')]
    pallas_call x0 -> x1, Pallas kernels: none -> 26.2 us  [shards(): pl.pallas_call(functools.partial(kernel, sizes), out_shape=(big, jax.Shap...]
    unnamed x23 -> x27, local copies, waits for them, and re-layouts: 1.53 us -> 13.4 us
    dot_general x5 -> x0, matrix products: 7.21 us -> none  [the longest x1 2.21 us: shards(): lax.dot_general(merged, p_factor, (((0,), (0,)), ((), ())), precision=HIG...]
  transfers between devices with their start and end apart: 1 -> 0, of which waited for: 1 -> 0; matrix products, arithmetic and copies ran while one was open for 0% -> 0% of each run, Pallas kernels for 0% -> 0%
where the time goes in v1:
time: 40.7 us; the launch traced here: 40.2 us
  Pallas kernels  26.2 us (64%)
  local copies, waits for them, and re-layouts  13.4 us (33%)
  between operations  0.67 us (2%)
    pallas_call x1, Pallas kernels, shards(): pl.pallas_call(functools.partial(kernel, sizes), out_shape=(big, jax.Shap...  26.2 us
    unnamed x27, local copies, waits for them, and re-layouts  13.4 us

profile of v1, /device:TPU:0, one launch (start us, length us, event | category | flops | bytes accessed | tf_op | source)
XLA Modules:
  0.0 40.2 jit_solution(9071643811510220268)
XLA Ops:
  0.6 0.0 copy-start.5
  0.6 0.7 %copy-done.5 = f32[1,32,32]{2,1,0:T(8,128)S(1)} copy-done((f32[1,32,32]{2,1,0:T(8,128)S(1)}, f32[1,32,32]{2,1,0:T(8,128)}, u32[]{:S(2)}) %copy-start.5) | copy-done | bytes 4120
  1.4 0.0 copy-start
  1.4 1.1 %copy-done = f32[1,1,192,768]{3,2,1,0:T(8,128)S(1)} copy-done((f32[1,1,192,768]{3,2,1,0:T(8,128)S(1)}, f32[1,1,192,768]{3,2,1,0:T(8,128)}, u32[]{:S(2)}) %copy-start) | copy-done | bytes 589848
  2.4 0.0 copy-start.1
  2.4 1.1 %copy-done.1 = f32[1,192,768]{2,1,0:T(8,128)S(1)} copy-done((f32[1,192,768]{2,1,0:T(8,128)S(1)}, f32[1,192,768]{2,1,0:T(8,128)}, u32[]{:S(2)}) %copy-start.1) | copy-done | bytes 589848
  3.5 0.0 copy-start.2
  3.5 1.1 %copy-done.2 = f32[1,192,768]{2,1,0:T(8,128)S(1)} copy-done((f32[1,192,768]{2,1,0:T(8,128)S(1)}, f32[1,192,768]{2,1,0:T(8,128)}, u32[]{:S(2)}) %copy-start.2) | copy-done | bytes 589848
  4.5 0.0 copy-start.3
  4.6 1.0 %copy-done.3 = bf16[1,1,192,768]{3,2,1,0:T(8,128)(2,1)S(1)} copy-done((bf16[1,1,192,768]{3,2,1,0:T(8,128)(2,1)S(1)}, bf16[1,1,192,768]{3,2,1,0:T(8,128)(2,1)}, u32[]{:S(2)}) %copy-start.3) | copy-done | bytes 294936
  5.5 0.0 copy-start.4
  5.5 0.9 %copy-done.4 = f32[1,768,32]{1,2,0:T(8,128)S(1)} copy-done((f32[1,768,32]{1,2,0:T(8,128)S(1)}, f32[1,768,32]{1,2,0:T(8,128)}, u32[]{:S(2)}) %copy-start.4) | copy-done | bytes 98328
  6.4 0.0 copy-start.6
  6.4 0.7 %copy-done.6 = f32[1,32,32]{2,1,0:T(8,128)S(1)} copy-done((f32[1,32,32]{2,1,0:T(8,128)S(1)}, f32[1,32,32]{2,1,0:T(8,128)}, u32[]{:S(2)}) %copy-start.6) | copy-done | bytes 4120
  7.1 0.0 copy-start.7
  7.1 0.7 %copy-done.7 = f32[1,1,3,192]{3,1,2,0:T(1,128)S(1)} copy-done((f32[1,1,3,192]{3,1,2,0:T(1,128)S(1)}, f32[1,1,3,192]{3,1,2,0:T(1,128)}, u32[]{:S(2)}) %copy-start.7) | copy-done | bytes 2328
  7.8 0.0 copy-start.8
  7.8 0.7 %copy-done.8 = f32[1,3,192]{2,0,1:T(1,128)S(1)} copy-done((f32[1,3,192]{2,0,1:T(1,128)S(1)}, f32[1,3,192]{2,0,1:T(1,128)}, u32[]{:S(2)}) %copy-start.8) | copy-done | bytes 2328
  8.5 0.0 copy-start.9
  8.5 0.7 %copy-done.9 = f32[1,3,192]{2,0,1:T(1,128)S(1)} copy-done((f32[1,3,192]{2,0,1:T(1,128)S(1)}, f32[1,3,192]{2,0,1:T(1,128)}, u32[]{:S(2)}) %copy-start.9) | copy-done | bytes 2328
  9.2 26.2 %shard_map.153 = (f32[192,768]{1,0:T(8,128)S(1)}, f32[32,192]{1,0:T(8,128)S(1)}, f32[32,768]{1,0:T(8,128)S(1)}, f32[192,768]{1,0:T(8,128)S(1)}, f32[192,768]{1,0...) custom-call(bf16[192,768]{1,0:T(8,128)(2,1)S(1)} %bitcast.29, f32[192,768]{1,0:T(8,128)S(1)} %bitcast.26, ...), custom_call_target="tpu_custom_call" | custom-call | tf_op jit(solution)/shard_map/pallas_call | solution.py:324
  35.4 0.8 %copy.24 = f32[1,1,192,768]{3,2,1,0:T(8,128)} copy(f32[1,1,192,768]{3,2,1,0:T(8,128)S(1)} %bitcast.25) | data formatting | bytes 1179648
  36.2 0.6 %copy.25 = f32[1,192,32]{1,2,0:T(8,128)} copy(f32[1,192,32]{1,2,0:T(8,128)S(1)} %bitcast.32) | data formatting | bytes 49152
  36.8 0.6 %copy.26 = f32[1,768,32]{1,2,0:T(8,128)} copy(f32[1,768,32]{1,2,0:T(8,128)S(1)} %bitcast.31) | data formatting | bytes 196608
  37.4 0.8 %copy.27 = f32[1,192,768]{2,1,0:T(8,128)} copy(f32[1,192,768]{2,1,0:T(8,128)S(1)} %bitcast.24) | data formatting | bytes 1179648
  38.2 0.8 %copy.28 = f32[1,192,768]{2,1,0:T(8,128)} copy(f32[1,192,768]{2,1,0:T(8,128)S(1)} %bitcast.23) | data formatting | bytes 1179648
  39.1 0.6 %copy.29 = f32[1,3,192]{2,0,1:T(1,128)} copy(f32[1,3,192]{2,0,1:T(1,128)S(1)} %bitcast.36) | data formatting | bytes 4608
  39.6 0.6 %copy.30 = f32[1,3,192]{2,0,1:T(1,128)} copy(f32[1,3,192]{2,0,1:T(1,128)S(1)} %bitcast.35) | data formatting | bytes 4608
Async XLA Ops:
  0.6 0.7 %copy-start.5 = (f32[1,32,32]{2,1,0:T(8,128)S(1)}, f32[1,32,32]{2,1,0:T(8,128)}, u32[]{:S(2)}) copy-start(f32[1,32,32]{2,1,0:T(8,128)} %param.13) | copy-start | bytes 12292
  1.4 1.1 %copy-start = (f32[1,1,192,768]{3,2,1,0:T(8,128)S(1)}, f32[1,1,192,768]{3,2,1,0:T(8,128)}, u32[]{:S(2)}) copy-start(f32[1,1,192,768]{3,2,1,0:T(8,128)} %param.11) | copy-start | bytes 1769476
  2.4 1.1 %copy-start.1 = (f32[1,192,768]{2,1,0:T(8,128)S(1)}, f32[1,192,768]{2,1,0:T(8,128)}, u32[]{:S(2)}) copy-start(f32[1,192,768]{2,1,0:T(8,128)} %param.15) | copy-start | bytes 1769476
  3.5 1.1 %copy-start.2 = (f32[1,192,768]{2,1,0:T(8,128)S(1)}, f32[1,192,768]{2,1,0:T(8,128)}, u32[]{:S(2)}) copy-start(f32[1,192,768]{2,1,0:T(8,128)} %param.16) | copy-start | bytes 1769476
  4.5 1.0 %copy-start.3 = (bf16[1,1,192,768]{3,2,1,0:T(8,128)(2,1)S(1)}, bf16[1,1,192,768]{3,2,1,0:T(8,128)(2,1)}, u32[]{:S(2)}) copy-start(bf16[1,1,192,768]{3,2,1,0:T(8,128)(2,1)} %param.10) | copy-start | bytes 884740
  5.5 0.9 %copy-start.4 = (f32[1,768,32]{1,2,0:T(8,128)S(1)}, f32[1,768,32]{1,2,0:T(8,128)}, u32[]{:S(2)}) copy-start(f32[1,768,32]{1,2,0:T(8,128)} %param.12) | copy-start | bytes 294916
  6.4 0.7 %copy-start.6 = (f32[1,32,32]{2,1,0:T(8,128)S(1)}, f32[1,32,32]{2,1,0:T(8,128)}, u32[]{:S(2)}) copy-start(f32[1,32,32]{2,1,0:T(8,128)} %param.14) | copy-start | bytes 12292
  7.1 0.7 %copy-start.7 = (f32[1,1,3,192]{3,1,2,0:T(1,128)S(1)}, f32[1,1,3,192]{3,1,2,0:T(1,128)}, u32[]{:S(2)}) copy-start(f32[1,1,3,192]{3,1,2,0:T(1,128)} %param.17) | copy-start | bytes 6916
  7.8 0.7 %copy-start.8 = (f32[1,3,192]{2,0,1:T(1,128)S(1)}, f32[1,3,192]{2,0,1:T(1,128)}, u32[]{:S(2)}) copy-start(f32[1,3,192]{2,0,1:T(1,128)} %param.18) | copy-start | bytes 6916
  8.5 0.7 %copy-start.9 = (f32[1,3,192]{2,0,1:T(1,128)S(1)}, f32[1,3,192]{2,0,1:T(1,128)}, u32[]{:S(2)}) copy-start(f32[1,3,192]{2,0,1:T(1,128)} %param.19) | copy-start | bytes 6916

commit v2 on v1

--- a/solution.py
+++ b/solution.py
@@ -44,10 +44,10 @@
 def kernel(
     sizes,
     g_hbm, e_hbm, qt_hbm, pr_hbm, qr_hbm, m_hbm, w_hbm, vg_hbm, vm_hbm, vp_hbm,
-    eo_hbm, pt_hbm, qf_hbm, mo_hbm, wo_hbm, vmo_hbm, vpo_hbm,
+    eo_v, pf_v, qf_v, mo_v, wo_v, vmo_v, vpo_v,
     g_v, e_v, qt_v, pr_v, qr_v, m_v, w_v, vm_v, vp_v,
-    hi_v, lo_v, pbuf, vbuf, qpart, rbuf, qfull, sbuf, pf_v, qf_v,
-    in_sem, out_sem, psend, precv, vsend, vrecv, rsend, rrecv, asend, arecv, ssend, srecv,
+    hi_v, lo_v, pbuf, vbuf, qpart, rbuf, qfull, sbuf,
+    in_sem, psend, precv, vsend, vrecv, rsend, rrecv, asend, arecv, ssend, srecv,
 ):
     n_dp, n_t, n_s = sizes
     n = n_dp * n_t
@@ -172,8 +172,6 @@
         send_chunk(k)
 
     pf_v[...] = pf
-    p_out = pltpu.make_async_copy(pf_v, pt_hbm, out_sem.at[0])
-    p_out.start()
     left = mm(q_root_left, right_parts(pf)).T / n_dp
     left = left_parts(left)
 
@@ -186,9 +184,7 @@
         v_sum = lax.fori_loop(1, n_dp, lambda i, acc: acc + vbuf[i], vbuf[0])
     ins[7].wait()
     v_new = 0.9 * vm_v[...] + v_sum / n_dp
-    vm_v[...] = v_new
-    v_out = pltpu.make_async_copy(vm_v, vmo_hbm, out_sem.at[1])
-    v_out.start()
+    vmo_v[...] = v_new
     v_square = jnp.sum(v_new * v_new)
 
     @pl.when(owns)
@@ -234,8 +230,7 @@
         q_parts.append(right)
         approx = mm(left, right)
         new = 0.9 * m_v[:, cols] + approx
-        m_v[:, cols] = new
-        e_v[:, cols] = e_v[:, cols] - approx
+        mo_v[:, cols] = new
         square = new * new
         for j in range(2):
             squares = squares + jnp.sum(
@@ -253,15 +248,11 @@
             sbuf.at[slot], sbuf.at[slot], ssend, srecv,
             device_id=(dp, lax.rem(peer, n_t), peer // n_t), device_id_type=MESH,
         ).start()
-    m_out = pltpu.make_async_copy(m_v, mo_hbm, out_sem.at[2])
-    m_out.start()
-    e_out = pltpu.make_async_copy(e_v, eo_hbm, out_sem.at[3])
-    e_out.start()
     q_root_t = left_parts(qr_v[...].T)
     for c in range(width // block):
-        qf_v[:, pl.ds(c * block, block)] = mm(q_root_t, q_parts[c])
-    q_out = pltpu.make_async_copy(qf_v, qf_hbm, out_sem.at[4])
-    q_out.start()
+        cols = pl.ds(c * block, block)
+        eo_v[:, cols] = e_v[:, cols] - mm(left, q_parts[c])
+        qf_v[:, cols] = mm(q_root_t, q_parts[c])
     ins[8].wait()
     ins[9].wait()
 
@@ -273,19 +264,8 @@
     total = jnp.sum(jnp.sum(total_tile, axis=1, keepdims=True), axis=0, keepdims=True)
     count = n_s * (width * width + 3 * width)
     scale = 0.05 / jnp.sqrt(total / count + 1e-06)
-    outs = [p_out, v_out, m_out, e_out, q_out]
-    pieces = 4
-    step = rows // pieces
-    for i in range(pieces):
-        part = pl.ds(i * step, step)
-        w_v[part, :] = w_v[part, :] - scale * m_v[part, :]
-        copy = pltpu.make_async_copy(w_v.at[part], wo_hbm.at[part], out_sem.at[5 + i])
-        copy.start()
-        outs.append(copy)
-    vp_v[...] = vp_v[...] - scale.reshape(1, 1, 1) * vm_v[...]
-    copy = pltpu.make_async_copy(vp_v, vpo_hbm, out_sem.at[5 + pieces])
-    copy.start()
-    outs.append(copy)
+    wo_v[...] = w_v[...] - scale * mo_v[...]
+    vpo_v[...] = vp_v[...] - scale.reshape(1, 1, 1) * vmo_v[...]
 
     pltpu.make_async_copy(pbuf.at[others], pbuf.at[others], psend).wait()
     pltpu.make_async_copy(vbuf.at[others], vbuf.at[others], vsend).wait()
@@ -302,7 +282,15 @@
     def _():
         pltpu.make_async_copy(qfull, qfull, rsend).wait()
 
-    for copy in outs:
+
+def write(count, *refs):
+    sems = refs[2 * count]
+    copies = [
+        pltpu.make_async_copy(refs[i], refs[count + i], sems.at[i]) for i in range(count)
+    ]
+    for copy in copies:
+        copy.start()
+    for copy in copies:
         copy.wait()
 
 
@@ -316,24 +304,30 @@
     vecs, entries = vec_params.shape[1:]
     n = n_dp * n_t
     chunks = (rank // CHUNK_ROWS) * (width // CHUNK_COLS)
-    big = jax.ShapeDtypeStruct((rows, width), F32)
-    vec = jax.ShapeDtypeStruct((vecs, 1, entries), F32)
+    big = (rows, width)
+    vec = (vecs, 1, entries)
+    shapes = (big, (rank, rows), (rank, width), big, big, vec, vec)
     any_space = pl.BlockSpec(memory_space=pl.ANY)
+    in_vmem = pl.BlockSpec(memory_space=pltpu.VMEM)
     dma = pltpu.SemaphoreType.DMA
     vmem = pltpu.VMEM
+    args = (
+        grads[0, 0],
+        errors[0, 0],
+        q_prev[0].T,
+        p_root[0],
+        q_root[0],
+        momentum[0],
+        weights[0],
+        vec_grads[0, 0][:, None, :],
+        vec_momentum[0][:, None, :],
+        vec_params[0][:, None, :],
+    )
     outs = pl.pallas_call(
         functools.partial(kernel, sizes),
-        out_shape=(
-            big,
-            jax.ShapeDtypeStruct((rank, rows), F32),
-            jax.ShapeDtypeStruct((rank, width), F32),
-            big,
-            big,
-            vec,
-            vec,
-        ),
-        in_specs=[pl.BlockSpec(memory_space=pltpu.HBM)] * 10,
-        out_specs=(any_space,) * 7,
+        out_shape=tuple(vmem(shape, F32) for shape in shapes),
+        in_specs=[any_space] * 10,
+        out_specs=(in_vmem,) * 7,
         scratch_shapes=[
             vmem((rows, width), BF16),
             vmem((rows, width), F32),
@@ -352,27 +346,20 @@
             vmem((n, CHUNK_ROWS, CHUNK_COLS), F32),
             vmem((chunks, CHUNK_ROWS, CHUNK_COLS), F32),
             vmem((n_t * n_s, 8, 128), F32),
-            vmem((rank, rows), F32),
-            vmem((rank, width), F32),
-            dma((10,)),
             dma((10,)),
         ]
         + [dma(())] * 10,
         compiler_params=pltpu.CompilerParams(
             collective_id=0, has_side_effects=True, vmem_limit_bytes=48 * 1024 * 1024
         ),
-    )(
-        grads[0, 0],
-        errors[0, 0],
-        q_prev[0].T,
-        p_root[0],
-        q_root[0],
-        momentum[0],
-        weights[0],
-        vec_grads[0, 0][:, None, :],
-        vec_momentum[0][:, None, :],
-        vec_params[0][:, None, :],
-    )
+    )(*(pltpu.with_memory_space_constraint(arg, pltpu.HBM) for arg in args))
+    outs = pl.pallas_call(
+        functools.partial(write, 7),
+        out_shape=tuple(pltpu.HBM(shape, F32) for shape in shapes),
+        in_specs=[in_vmem] * 7,
+        out_specs=(any_space,) * 7,
+        scratch_shapes=[dma((7,))],
+    )(*(pltpu.with_memory_space_constraint(out, pltpu.VMEM) for out in outs))
     errors_out, p_factor, q_factor, momentum_out, weights_out, vec_momentum_out, vec_params_out = outs
     return (
         errors_out[None, None],

time: 40.7 us -> 26.7 us (0.66)
  local copies, waits for them, and re-layouts: 13.4 us -> 0 us
    unnamed x27 -> x0, local copies, waits for them, and re-layouts: 13.4 us -> none
    pallas_call x1 -> x2, Pallas kernels: 26.2 us -> 25.9 us  [the longest x1 24.6 us: shards(): pl.pallas_call(functools.partial(kernel, sizes), out_shape=tuple((vmem(sh...]
where the time goes in v2:
time: 26.7 us; the launch traced here: 26.6 us
  Pallas kernels  25.9 us (97%)
  between operations  0.64 us (2%)
    pallas_call x1, Pallas kernels, shards(): pl.pallas_call(functools.partial(kernel, sizes), out_shape=tuple((vmem(sh...  24.6 us
    pallas_call x1, Pallas kernels, shards(): pl.pallas_call(functools.partial(write, 7), out_shape=tuple((pltpu.HBM(sh...  1.32 us

profile of v2, /device:TPU:0, one launch (start us, length us, event | category | flops | bytes accessed | tf_op | source)
XLA Modules:
  0.0 26.6 jit_solution(13234541027637493056)
XLA Ops:
  0.6 24.6 %shard_map.153 = (f32[192,768]{1,0:T(8,128)S(1)}, f32[32,192]{1,0:T(8,128)S(1)}, f32[32,768]{1,0:T(8,128)S(1)}, f32[192,768]{1,0:T(8,128)S(1)}, f32[192,768]{1,0...) custom-call(bf16[192,768]{1,0:T(8,128)(2,1)} %bitcast.26, f32[192,768]{1,0:T(8,128)} %bitcast.23, ...), custom_call_target="tpu_custom_call" | custom-call | tf_op jit(solution)/shard_map/pallas_call | solution.py:326
  25.2 1.3 %shard_map.154 = (f32[192,768]{1,0:T(8,128)}, f32[32,192]{1,0:T(8,128)}, f32[32,768]{1,0:T(8,128)}, f32[192,768]{1,0:T(8,128)}, f32[192,768]{1,0:T(8,128)}, /*index=5*/f32[3,1,192]{2,1,0:T(1,128)}, f32[3,1,192]{2,1,0:T(1,128)}) custom-call(f32[192,768]{1,0:T(8,128)S(1)} %get-tuple-element.21.refs_0_, f32[32,192]{1,0:T(8,128)S(1)} %get-tuple-element.22.refs_1_, ...), custom_call_target="tpu_custom_call" | custom-call | tf_op jit(solution)/shard_map/pallas_call | solution.py:356

commit v3 on v2

--- a/solution.py
+++ b/solution.py
@@ -80,21 +80,21 @@
     ]
 
     barrier = pltpu.get_barrier_semaphore()
-
-    def greet_group(i):
-        peer = lax.rem(me + 1 + i, n)
+    slot = sc * n_t + tn
+
+    def greet_line(i):
         pl.semaphore_signal(
-            barrier, inc=1, device_id=(peer // n_t, lax.rem(peer, n_t), sc), device_id_type=MESH
+            barrier, inc=1, device_id=(lax.rem(dp + 1 + i, n_dp), tn, sc), device_id_type=MESH
         )
 
-    def greet_section(i):
-        other = lax.rem(sc + 1 + i // n_t, n_s)
+    def greet_plane(i):
+        peer = lax.rem(slot + 1 + i, group)
         pl.semaphore_signal(
-            barrier, inc=1, device_id=(dp, i % n_t, other), device_id_type=MESH
+            barrier, inc=1, device_id=(dp, lax.rem(peer, n_t), peer // n_t), device_id_type=MESH
         )
 
-    each(n - 1, greet_group)
-    each((n_s - 1) * n_t, greet_section)
+    each(n_dp - 1, greet_line)
+    each(group - 1, greet_plane)
 
     ins[2].wait()
     q_hi, q_lo = split(qt_v[...])
@@ -109,7 +109,7 @@
     second = mm(q_hi, lo_v[...], ((1,), (1,)))
     pbuf[dp] = first[:rank] + first[rank:] + second
 
-    pl.semaphore_wait(barrier, n - 1 + (n_s - 1) * n_t)
+    pl.semaphore_wait(barrier, n_dp - 1 + group - 1)
     ins[5].wait()
 
     def send_p(i):
@@ -125,7 +125,6 @@
         ).start()
 
     each(n_dp - 1, send_p)
-    each(n_dp - 1, send_v)
 
     ins[3].wait()
     ins[4].wait()
@@ -168,24 +167,14 @@
         first = mm(pf_both, hi_v[:, cols])
         second = mm(pf_hi, lo_v[:, cols])
         qpart[:, cols] = first[:rank] + first[rank:] + second
-    for k in range(chunks):
-        send_chunk(k)
+        for r in range(rank // CHUNK_ROWS):
+            for j in range(2):
+                send_chunk(r * col_chunks + 2 * c + j)
+    each(n_dp - 1, send_v)
 
     pf_v[...] = pf
     left = mm(q_root_left, right_parts(pf)).T / n_dp
     left = left_parts(left)
-
-    pltpu.make_async_copy(vbuf.at[others], vbuf.at[others], vrecv).wait()
-    if n_dp <= 16:
-        v_sum = vbuf[0]
-        for i in range(1, n_dp):
-            v_sum = v_sum + vbuf[i]
-    else:
-        v_sum = lax.fori_loop(1, n_dp, lambda i, acc: acc + vbuf[i], vbuf[0])
-    ins[7].wait()
-    v_new = 0.9 * vm_v[...] + v_sum / n_dp
-    vmo_v[...] = v_new
-    v_square = jnp.sum(v_new * v_new)
 
     @pl.when(owns)
     def _():
@@ -200,13 +189,19 @@
         qfull[mine] = q_sum
 
         def send_sum(i):
-            peer = lax.rem(me + 1 + i, n)
+            peer = lax.rem(2 * n - 1 - me + i, n)
+
+            @pl.when(peer != me)
+            def _():
+                send_sum_to(peer)
+
+        def send_sum_to(peer):
             pltpu.make_async_remote_copy(
                 qfull.at[mine], qfull.at[mine], asend, arecv,
                 device_id=(peer // n_t, lax.rem(peer, n_t), sc), device_id_type=MESH,
             ).start()
 
-        each(n - 1, send_sum)
+        each(n, send_sum)
         got = pl.ds(0, chunks - 1)
         pltpu.make_async_copy(qfull.at[got], qfull.at[got], arecv).wait()
 
@@ -236,11 +231,22 @@
             squares = squares + jnp.sum(
                 square[:, j * 128 : (j + 1) * 128].reshape(rows // 8, 8, 128), axis=0
             )
+    pltpu.make_async_copy(vbuf.at[others], vbuf.at[others], vrecv).wait()
+    if n_dp <= 16:
+        v_sum = vbuf[0]
+        for i in range(1, n_dp):
+            v_sum = v_sum + vbuf[i]
+    else:
+        v_sum = lax.fori_loop(1, n_dp, lambda i, acc: acc + vbuf[i], vbuf[0])
+    ins[7].wait()
+    v_new = 0.9 * vm_v[...] + v_sum / n_dp
+    vmo_v[...] = v_new
+    v_square = jnp.sum(v_new * v_new)
+
     corner = jnp.logical_and(
         lax.broadcasted_iota(jnp.int32, (8, 128), 0) == 0,
         lax.broadcasted_iota(jnp.int32, (8, 128), 1) == 0,
     )
-    slot = sc * n_t + tn
     sbuf[slot] = squares + jnp.where(corner, v_square, 0.0)
     for i in range(1, group):
         peer = lax.rem(slot + i, group)

time: 26.7 us -> 25.6 us (0.959)
  Pallas kernels: 25.9 us -> 24.8 us
    pallas_call x1, Pallas kernels: 24.6 us -> 23.5 us  [shards(): pl.pallas_call(functools.partial(kernel, sizes), out_shape=tuple((vmem(sh...]
where the time goes in v3:
time: 25.6 us; the launch traced here: 25.4 us
  Pallas kernels  24.8 us (97%)
  between operations  0.64 us (2%)
    pallas_call x1, Pallas kernels, shards(): pl.pallas_call(functools.partial(kernel, sizes), out_shape=tuple((vmem(sh...  23.5 us
    pallas_call x1, Pallas kernels, shards(): pl.pallas_call(functools.partial(write, 7), out_shape=tuple((pltpu.HBM(sh...  1.32 us

profile of v3, /device:TPU:0, one launch (start us, length us, event | category | flops | bytes accessed | tf_op | source)
XLA Modules:
  0.0 25.4 jit_solution(4370509793199173216)
XLA Ops:
  0.6 23.5 %shard_map.153 = (f32[192,768]{1,0:T(8,128)S(1)}, f32[32,192]{1,0:T(8,128)S(1)}, f32[32,768]{1,0:T(8,128)S(1)}, f32[192,768]{1,0:T(8,128)S(1)}, f32[192,768]{1,0...) custom-call(bf16[192,768]{1,0:T(8,128)(2,1)} %bitcast.26, f32[192,768]{1,0:T(8,128)} %bitcast.23, ...), custom_call_target="tpu_custom_call" | custom-call | tf_op jit(solution)/shard_map/pallas_call | solution.py:332
  24.1 1.3 %shard_map.154 = (f32[192,768]{1,0:T(8,128)}, f32[32,192]{1,0:T(8,128)}, f32[32,768]{1,0:T(8,128)}, f32[192,768]{1,0:T(8,128)}, f32[192,768]{1,0:T(8,128)}, /*index=5*/f32[3,1,192]{2,1,0:T(1,128)}, f32[3,1,192]{2,1,0:T(1,128)}) custom-call(f32[192,768]{1,0:T(8,128)S(1)} %get-tuple-element.21.refs_0_, f32[32,192]{1,0:T(8,128)S(1)} %get-tuple-element.22.refs_1_, ...), custom_call_target="tpu_custom_call" | custom-call | tf_op jit(solution)/shard_map/pallas_call | solution.py:362

commit v4 on v3

--- a/solution.py
+++ b/solution.py
@@ -10,7 +10,7 @@
 F32 = jnp.float32
 BF16 = jnp.bfloat16
 MESH = pl.DeviceIdType.MESH
-CHUNK_ROWS = 16
+CHUNK_ROWS = 32
 CHUNK_COLS = 128
 
 

time: 25.6 us -> 26.3 us (1.027)
  Pallas kernels: 24.8 us -> 25.5 us
    pallas_call x1, Pallas kernels: 23.5 us -> 24.2 us  [shards(): pl.pallas_call(functools.partial(kernel, sizes), out_shape=tuple((vmem(sh...]
where the time goes in v4:
time: 26.3 us; the launch traced here: 26.1 us
  Pallas kernels  25.5 us (97%)
  between operations  0.64 us (2%)
    pallas_call x1, Pallas kernels, shards(): pl.pallas_call(functools.partial(kernel, sizes), out_shape=tuple((vmem(sh...  24.2 us
    pallas_call x1, Pallas kernels, shards(): pl.pallas_call(functools.partial(write, 7), out_shape=tuple((pltpu.HBM(sh...  1.32 us

profile of v4, /device:TPU:0, one launch (start us, length us, event | category | flops | bytes accessed | tf_op | source)
XLA Modules:
  0.0 26.1 jit_solution(14526848025749821354)
XLA Ops:
  0.6 24.2 %shard_map.153 = (f32[192,768]{1,0:T(8,128)S(1)}, f32[32,192]{1,0:T(8,128)S(1)}, f32[32,768]{1,0:T(8,128)S(1)}, f32[192,768]{1,0:T(8,128)S(1)}, f32[192,768]{1,0...) custom-call(bf16[192,768]{1,0:T(8,128)(2,1)} %bitcast.26, f32[192,768]{1,0:T(8,128)} %bitcast.23, ...), custom_call_target="tpu_custom_call" | custom-call | tf_op jit(solution)/shard_map/pallas_call | solution.py:332
  24.8 1.3 %shard_map.154 = (f32[192,768]{1,0:T(8,128)}, f32[32,192]{1,0:T(8,128)}, f32[32,768]{1,0:T(8,128)}, f32[192,768]{1,0:T(8,128)}, f32[192,768]{1,0:T(8,128)}, /*index=5*/f32[3,1,192]{2,1,0:T(1,128)}, f32[3,1,192]{2,1,0:T(1,128)}) custom-call(f32[192,768]{1,0:T(8,128)S(1)} %get-tuple-element.21.refs_0_, f32[32,192]{1,0:T(8,128)S(1)} %get-tuple-element.22.refs_1_, ...), custom_call_target="tpu_custom_call" | custom-call | tf_op jit(solution)/shard_map/pallas_call | solution.py:362
